TPU v7x, 512 devices: a whole 4x8x8 slice. The times are simulated.
512 devices in a mesh: dp: 8 (over z_hi, x), expert: 64 (over z_lo, y, core).
Axes of the slice: x: 4, y: 8, z: 8 (z_hi: 2, z_lo: 4; z = z_hi * 4 + z_lo), core: 2. Of those that a mesh axis runs over, the one named last changes fastest.
Arguments:
- features: bfloat16 [8192, 3584], P('expert', 'dp'), may hold values from -6 to 6
- upstream: bfloat16 [8192, 3584], P('expert', 'dp'), may hold values from -6 to 6
- expert_ids: int32 [8192, 8], P('expert'), may hold values from 0 to 63, all different within a row
- gate_probs: float32 [8192, 8], P('expert'), may hold values from 0.02 to 0.5
- capacity: int32 [64], replicated, may hold values from 1 to 16, as said below
- up_weight: bfloat16 [64, 3584, 1024], P('expert', 'dp'), may hold values from -5 to 5
- down_weight: bfloat16 [64, 1024, 3584], P('expert', None, 'dp'), may hold values from -5 to 5
- round_noise: bfloat16 [64, 3584, 1024], P('expert', 'dp'), may hold values from 0 to 1
Outputs:
- mixed: bfloat16 [8192, 3584], P('expert', 'dp')
- grad_tokens: bfloat16 [8192, 3584], P('expert', 'dp')
- new_up: bfloat16 [64, 3584, 1024], P('expert', 'dp')
- new_down: bfloat16 [64, 1024, 3584], P('expert', None, 'dp')
Inputs may be any that keep to these rules, and one draw needn't show every extreme that they name: Experts 64/2 .. 63 have capacity 12 + 1 to 16; experts 0 .. 31 have capacity 12 - 4 or less; some expert has exactly 16, and some exactly 8.
All inputs are finite; a program needn't handle non-finite values.
Results may differ from a plain program's by a relative error of at most 0.025.
Values may be sent and summed in bfloat16 or wider, within the bound.
A program may use at most 64 MiB of HBM per device.

v0:
```python
import jax
import jax.numpy as jnp
from jax import lax
from jax.sharding import PartitionSpec as P

D = 3584
FFN = 1024
SLOT_BLOCK = 4
CAP = 12


step_size = 4.0
noise_width = 0.25


def shifted(block, axis, distance):
    devices = range(lax.axis_size(axis))
    route = [(i - distance, i) for i in devices if i - distance in devices]
    return lax.ppermute(block, axis, route)


def silu_slope(pre_act):
    sigmoid = jax.nn.sigmoid(pre_act)
    return sigmoid * (1.0 + pre_act * (1.0 - sigmoid))


def stochastic(weights, grads, noise):
    target = weights.astype(jnp.float32) - step_size * grads
    spacing = noise_width * jnp.abs(target)
    return (target + (noise.astype(jnp.float32) - 0.5) * spacing).astype(jnp.bfloat16)


def dp_total(lead_terms, tail_terms):
    return (
        lax.psum(lead_terms.astype(jnp.bfloat16), "dp").astype(jnp.float32),
        lax.psum(tail_terms.astype(jnp.bfloat16), "dp").astype(jnp.float32),
    )


def project_in(row_block, weight, scale):
    return jnp.dot(row_block, weight, preferred_element_type=jnp.float32) * scale


def project_back(row_block, weight, scale):
    return (
        lax.dot_general(
            row_block, weight, (((1,), (1,)), ((), ())), preferred_element_type=jnp.float32
        )
        * scale
    )


def outer_sum(left_rows, right_rows, scale):
    return (
        lax.dot_general(
            left_rows, right_rows, (((0,), (0,)), ((), ())), preferred_element_type=jnp.float32
        )
        * scale
    )


def shards(
    features, upstream, expert_ids, gate_probs, capacity, up_weight, down_weight, round_noise
):
    experts_all = lax.axis_size("expert")
    my_index = lax.axis_index("expert")
    half_axis = experts_all // 2
    partner = (my_index + half_axis) % experts_all
    tok_count, top_count = expert_ids.shape
    local_feat = features.shape[1]
    up_scale = D ** (-0.5)
    down_scale = FFN ** (-0.5)
    flat_ids = expert_ids.reshape(-1)
    columns = jnp.arange(experts_all, dtype=jnp.int32)
    onehot = (flat_ids[:, None] == columns[None, :]).astype(jnp.int32)
    earlier = jnp.cumsum(onehot, axis=0) - onehot
    ranking = jnp.sum(earlier * onehot, axis=1)
    limits = jnp.sum(onehot * capacity[None, :], axis=1)
    kept = ranking < limits
    width = CAP
    lead_rows = CAP - SLOT_BLOCK
    spill = ranking >= CAP
    target = jnp.where(spill, (flat_ids + half_axis) % experts_all, flat_ids)
    position = jnp.where(spill, ranking - SLOT_BLOCK, ranking)
    slot_ids = jnp.where(kept, target * width + position, -1).reshape(tok_count, top_count)
    slot_range = jnp.arange(experts_all * width, dtype=jnp.int32)
    matches = slot_ids[:, :, None] == slot_range[None, None, :]
    picker = jnp.sum(matches.astype(jnp.int32), axis=1).astype(jnp.bfloat16)
    slot_prob = jnp.sum(jnp.where(matches, gate_probs[:, :, None], 0.0), axis=(0, 1))
    both_rows = jnp.concatenate([features, upstream], axis=1)
    gathered = jnp.einsum("ts,td->sd", picker, both_rows, preferred_element_type=jnp.float32)
    send_feat = gathered[:, :local_feat].astype(jnp.bfloat16)
    send_grad = (slot_prob[:, None] * gathered[:, local_feat:]).astype(jnp.bfloat16)
    send_feat = send_feat.reshape(experts_all, width, local_feat)
    send_grad = send_grad.reshape(experts_all, width, local_feat)
    recv_feat, recv_grad = (
        lax.all_to_all(send_feat, "expert", split_axis=0, concat_axis=0, tiled=True),
        lax.all_to_all(send_grad, "expert", split_axis=0, concat_axis=0, tiled=True),
    )
    up_own = up_weight[0]
    down_own = down_weight[0]
    helping = jnp.sum(jnp.where(columns == partner, capacity, 0)) > CAP
    up_copy, down_copy = shifted((up_weight, down_weight), "expert", -half_axis)
    up_tail = jnp.where(helping, up_copy[0], up_own)
    down_tail = jnp.where(helping, down_copy[0], down_own)
    lead_feat = recv_feat[:, :lead_rows].reshape(-1, local_feat)
    tail_feat = recv_feat[:, lead_rows:].reshape(-1, local_feat)
    lead_grad = recv_grad[:, :lead_rows].reshape(-1, local_feat)
    tail_grad = recv_grad[:, lead_rows:].reshape(-1, local_feat)
    lead_pre, tail_pre = dp_total(
        project_in(lead_feat, up_own, up_scale), project_in(tail_feat, up_tail, up_scale)
    )
    lead_act = jax.nn.silu(lead_pre).astype(jnp.bfloat16)
    tail_act = jax.nn.silu(tail_pre).astype(jnp.bfloat16)
    lead_out = project_in(lead_act, down_own, down_scale).astype(jnp.bfloat16)
    tail_out = project_in(tail_act, down_tail, down_scale).astype(jnp.bfloat16)
    lead_dact, tail_dact = dp_total(
        project_back(lead_grad, down_own, down_scale),
        project_back(tail_grad, down_tail, down_scale),
    )
    lead_dpre = (lead_dact * silu_slope(lead_pre)).astype(jnp.bfloat16)
    tail_dpre = (tail_dact * silu_slope(tail_pre)).astype(jnp.bfloat16)
    lead_dx = project_back(lead_dpre, up_own, up_scale).astype(jnp.bfloat16)
    tail_dx = project_back(tail_dpre, up_tail, up_scale).astype(jnp.bfloat16)
    out_slots = jnp.concatenate(
        [
            lead_out.reshape(experts_all, lead_rows, local_feat),
            tail_out.reshape(experts_all, -1, local_feat),
        ],
        axis=1,
    )
    dx_slots = jnp.concatenate(
        [
            lead_dx.reshape(experts_all, lead_rows, local_feat),
            tail_dx.reshape(experts_all, -1, local_feat),
        ],
        axis=1,
    )
    back_out, back_dx = (
        lax.all_to_all(out_slots, "expert", split_axis=0, concat_axis=0, tiled=True),
        lax.all_to_all(dx_slots, "expert", split_axis=0, concat_axis=0, tiled=True),
    )
    is_kept = slot_ids >= 0
    safe_slots = jnp.maximum(slot_ids, 0).reshape(-1)
    row_weight = jnp.where(is_kept, gate_probs, 0.0)
    out_rows = (
        jnp.take(back_out.reshape(-1, local_feat), safe_slots, axis=0)
        .reshape(tok_count, top_count, local_feat)
        .astype(jnp.float32)
    )
    mixed = jnp.sum(out_rows * row_weight[:, :, None], axis=1).astype(jnp.bfloat16)
    dx_rows = (
        jnp.take(back_dx.reshape(-1, local_feat), safe_slots, axis=0)
        .reshape(tok_count, top_count, local_feat)
        .astype(jnp.float32)
    )
    grad_tokens = jnp.sum(jnp.where(is_kept[:, :, None], dx_rows, 0.0), axis=1).astype(jnp.bfloat16)
    up_lead_grad = outer_sum(lead_feat, lead_dpre, up_scale)
    up_tail_grad = outer_sum(tail_feat, tail_dpre, up_scale)
    down_lead_grad = outer_sum(lead_act, lead_grad, down_scale)
    down_tail_grad = outer_sum(tail_act, tail_grad, down_scale)
    up_replica = jnp.where(helping, up_tail_grad, 0.0)
    down_replica = jnp.where(helping, down_tail_grad, 0.0)
    up_back, down_back = (
        shifted(up_replica.astype(jnp.bfloat16), "expert", half_axis).astype(up_replica.dtype),
        shifted(down_replica.astype(jnp.bfloat16), "expert", half_axis).astype(down_replica.dtype),
    )
    up_total = up_lead_grad + jnp.where(helping, 0.0, up_tail_grad) + up_back
    down_total = down_lead_grad + jnp.where(helping, 0.0, down_tail_grad) + down_back
    noise_own = round_noise[0]
    new_up = stochastic(up_own, up_total, noise_own)
    new_down = stochastic(down_own, down_total, noise_own.T)
    return (mixed, grad_tokens, new_up[None], new_down[None])


def solution(mesh):
    in_specs = (
        P("expert", "dp"),
        P("expert", "dp"),
        P("expert", None),
        P("expert", None),
        P(),
        P("expert", "dp", None),
        P("expert", None, "dp"),
        P("expert", "dp", None),
    )
    out_specs = (
        P("expert", "dp"),
        P("expert", "dp"),
        P("expert", "dp", None),
        P("expert", None, "dp"),
    )
    return jax.shard_map(shards, mesh=mesh, in_specs=in_specs, out_specs=out_specs, check_vma=False)
```

profile of v0, /device:TPU:65, one launch (start us, length us, event | category | flops | bytes accessed | tf_op | source)
XLA Modules:
  0.0 530.2 jit_solution(2290183015718349692)
XLA Ops:
  9.0 18.0 %reduce-window.6 = s32[64,8,128]{2,1,0:T(8,128)S(1)} reduce-window(s32[64,8,128]{2,1,0:T(8,128)S(1)} %fusion.48, s32[]{:T(128)} %constant.28.clone.1), window={size=1x1x128 pad=0_0x0_0x127_0}, to_apply=%region_0.1 | reduce-window | flops 8323072 | bytes 524292 | tf_op jit(solution)/shard_map/reduce-window
  31.5 13.4 %all-to-all-start = ((bf16[64,12,448]{2,1,0:T(8,128)(2,1)}), bf16[64,12,448]{2,1,0:T(8,128)(2,1)}, u32[]{:S(2)}, u32[]{:S(2)}) async-start(bf16[64,12,448]{2,1,0:T(8,128)(2,1)} %reshape.122), calls=%async_computation | async-start | bytes 2097152 | tf_op jit(solution)/shard_map/all_to_all | solution.py:97
  47.2 26.0 %all-to-all-done = bf16[64,12,448]{2,1,0:T(8,128)(2,1)} async-done(((bf16[64,12,448]{2,1,0:T(8,128)(2,1)}), bf16[64,12,448]{2,1,0:T(8,128)(2,1)}, u32[]{:S(2)}, u32[]{:S(2)}) %all-to-all-start) | async-done | bytes 688160 | tf_op jit(solution)/shard_map/all_to_all | solution.py:97
  73.2 6.1 %all-to-all-start.2 = ((bf16[64,12,448]{2,1,0:T(8,128)(2,1)}), bf16[64,12,448]{2,1,0:T(8,128)(2,1)S(1)}, u32[]{:S(2)}, u32[]{:S(2)}) async-start(bf16[64,12,448]{2,1,0:T(8,128)(2,1)} %reshape.129), calls=%async_computation.2 | async-start | bytes 2097152 | tf_op jit(solution)/shard_map/all_to_all | solution.py:98
  79.4 1.3 collective-permute-start.1
  80.7 1.3 collective-permute-start
  84.6 23.2 %all-to-all-done.2 = bf16[64,12,448]{2,1,0:T(8,128)(2,1)S(1)} async-done(((bf16[64,12,448]{2,1,0:T(8,128)(2,1)}), bf16[64,12,448]{2,1,0:T(8,128)(2,1)S(1)}, u32[]{:S(2)}, u32[]{:S(2)}) %all-to-all-start.2) | async-done | bytes 688160 | tf_op jit(solution)/shard_map/all_to_all | solution.py:98
  108.0 1.7 multiply_convert_fusion
  109.7 3.0 multiply_convert_fusion.1
  112.8 11.0 %collective-permute-done.1 = bf16[1,1024,448]{1,2,0:T(8,128)(2,1)} collective-permute-done((bf16[1,1024,448]{1,2,0:T(8,128)(2,1)S(1)}, bf16[1,1024,448]{1,2,0:T(8,128)(2,1)}, u32[]{:S(2)}, u32[]{:S(2)}) %collective-permute-start.1) | collective-permute-done | bytes 917536 | tf_op jit(solution)/shard_map/ppermute | solution.py:19
  123.8 2.4 fusion.18
  126.2 17.2 %collective-permute-done = bf16[1,448,1024]{2,1,0:T(8,128)(2,1)} collective-permute-done((bf16[1,448,1024]{2,1,0:T(8,128)(2,1)}, bf16[1,448,1024]{2,1,0:T(8,128)(2,1)}, u32[]{:S(2)}, u32[]{:S(2)}) %collective-permute-start) | collective-permute-done | bytes 917536 | tf_op jit(solution)/shard_map/ppermute | solution.py:19
  143.5 2.4 fusion.17
  146.9 210.7 %all-reduce.3.cloned.1.call-done = (bf16[256,1024]{1,0:T(8,128)(2,1)}, bf16[256,1024]{1,0:T(8,128)(2,1)}, bf16[512,1024]{1,0:T(8,128)(2,1)}, bf16[512,1024]{1,0:T(8,128)(2,1)}) async-done(((bf16[256,1024]{1,0:T(8,128)(2,1)}, bf16[256,1024]{1,0:T(8,128)(2,1)}, bf16[512,1024]{1,0:T(8,128)(2,1)}, bf16[512,1024]{1,0:T(8,128)(2,1)}), (bf16[256,1024]{1,0:T(8,128)(2,1)}, bf16[256,1024]{1,0:T(8,128)(2,1)}, ...) | async-done | bytes 3145744 | tf_op jit(solution)/shard_map/psum | solution.py:36
  357.6 2.5 fusion.22
  360.3 3.0 fusion.20
  364.7 13.8 %all-to-all-start.3 = ((bf16[64,12,448]{2,1,0:T(8,128)(2,1)}), bf16[64,12,448]{2,1,0:T(8,128)(2,1)S(1)}, u32[]{:S(2)}, u32[]{:S(2)}) async-start(bf16[64,12,448]{2,1,0:T(8,128)(2,1)} %pad_maximum_fusion.1), calls=%async_computation.3 | async-start | bytes 2097152 | tf_op jit(solution)/shard_map/all_to_all | solution.py:141
  378.5 3.5 select_convert_fusion.1
  382.1 5.3 collective-permute-start.2
  387.4 2.1 select_convert_fusion
  389.5 2.2 collective-permute-start.3
  391.7 1.7 fusion.19
  393.4 1.7 fusion.21
  396.6 1.3 pad_maximum_fusion
  397.9 9.0 %all-to-all-done.3 = bf16[64,12,448]{2,1,0:T(8,128)(2,1)S(1)} async-done(((bf16[64,12,448]{2,1,0:T(8,128)(2,1)}), bf16[64,12,448]{2,1,0:T(8,128)(2,1)S(1)}, u32[]{:S(2)}, u32[]{:S(2)}) %all-to-all-start.3) | async-done | bytes 688160 | tf_op jit(solution)/shard_map/all_to_all | solution.py:141
  406.9 45.4 %all-to-all-start.1 = ((bf16[64,12,448]{2,1,0:T(8,128)(2,1)}), bf16[64,12,448]{2,1,0:T(8,128)(2,1)S(1)}, u32[]{:S(2)}, u32[]{:S(2)}) async-start(bf16[64,12,448]{2,1,0:T(8,128)(2,1)} %pad_maximum_fusion), calls=%async_computation.1 | async-start | bytes 2097152 | tf_op jit(solution)/shard_map/all_to_all | solution.py:140
  452.3 49.3 %collective-permute-done.3 = bf16[1024,448]{0,1:T(8,128)(2,1)} collective-permute-done((bf16[1024,448]{0,1:T(8,128)(2,1)}, bf16[1024,448]{0,1:T(8,128)(2,1)}, u32[]{:S(2)}, u32[]{:S(2)}) %collective-permute-start.3) | collective-permute-done | bytes 917536 | tf_op jit(solution)/shard_map/ppermute | solution.py:19
  501.6 5.3 fusion.16
  506.9 4.4 fusion.15
  511.7 4.0 gather_fusion.1
  516.1 4.0 gather_fusion
  520.1 1.7 fusion.8
  (82 shorter events, 16.9 us)
Async XLA Ops:
  7.2 20.4 %copy-start.8 = (s32[64]{0:T(128)S(1)}, s32[64]{0:T(128)}, u32[]{:S(2)}) copy-start(s32[64]{0:T(128)} %param.14) | copy-start | bytes 772
  7.2 22.4 %copy-start.6 = (bf16[128,448]{0,1:T(8,128)(2,1)S(1)}, bf16[128,448]{0,1:T(8,128)(2,1)}, u32[]{:S(2)}) copy-start(bf16[128,448]{0,1:T(8,128)(2,1)} %param.11) | copy-start | bytes 344068
  7.2 22.4 %copy-start.7 = (bf16[128,448]{0,1:T(8,128)(2,1)S(1)}, bf16[128,448]{0,1:T(8,128)(2,1)}, u32[]{:S(2)}) copy-start(bf16[128,448]{0,1:T(8,128)(2,1)} %param.10) | copy-start | bytes 344068
  9.0 19.6 %copy-start.3 = (f32[128,8]{1,0:T(8,128)}, f32[128,8]{1,0:T(8,128)S(1)}, u32[]{:S(2)}) copy-start(f32[128,8]{1,0:T(8,128)S(1)} %copy.52) | copy-start | bytes 12292
  28.6 1.6 copy-start
  31.5 13.4 %copy-start.1 = (s32[128,8]{1,0:T(8,128)S(1)}, s32[128,8]{1,0:T(8,128)}, u32[]{:S(2)}) copy-start(s32[128,8]{1,0:T(8,128)} %copy-done) | copy-start | bytes 12292
  31.5 13.4 %copy-start.4 = (f32[128,8]{1,0:T(8,128)S(1)}, f32[128,8]{1,0:T(8,128)}, u32[]{:S(2)}) copy-start(f32[128,8]{1,0:T(8,128)} %copy-done.3) | copy-start | bytes 12292
  31.5 41.7 %all-to-all-start = ((bf16[64,12,448]{2,1,0:T(8,128)(2,1)}), bf16[64,12,448]{2,1,0:T(8,128)(2,1)}, u32[]{:S(2)}, u32[]{:S(2)}) async-start(bf16[64,12,448]{2,1,0:T(8,128)(2,1)} %reshape.122), calls=%async_computation | async-start | bytes 2097152 | tf_op jit(solution)/shard_map/all_to_all | solution.py:97
  45.9 33.5 %copy-start.13 = (bf16[1,1024,448]{1,2,0:T(8,128)(2,1)S(1)}, bf16[1,1024,448]{1,2,0:T(8,128)(2,1)}, u32[]{:S(2)}) copy-start(bf16[1,1024,448]{1,2,0:T(8,128)(2,1)} %param.16) | copy-start | bytes 2752516
  46.0 36.1 %copy-start.9 = (s32[64]{0:T(128)S(1)}, s32[64]{0:T(128)}, u32[]{:S(2)}) copy-start(s32[64]{0:T(128)} %param.14) | copy-start | bytes 772
  73.2 34.5 %all-to-all-start.2 = ((bf16[64,12,448]{2,1,0:T(8,128)(2,1)}), bf16[64,12,448]{2,1,0:T(8,128)(2,1)S(1)}, u32[]{:S(2)}, u32[]{:S(2)}) async-start(bf16[64,12,448]{2,1,0:T(8,128)(2,1)} %reshape.129), calls=%async_computation.2 | async-start | bytes 2097152 | tf_op jit(solution)/shard_map/all_to_all | solution.py:98
  79.4 278.2 %all-reduce.3.cloned.1.call-start = ((), (), s32[]{:S(2)}) async-start(), calls=%async_computation.4 | async-start | bytes 6291456 | tf_op jit(solution)/shard_map/psum | solution.py:36
  79.4 44.4 %collective-permute-start.1 = (bf16[1,1024,448]{1,2,0:T(8,128)(2,1)S(1)}, bf16[1,1024,448]{1,2,0:T(8,128)(2,1)}, u32[]{:S(2)}, u32[]{:S(2)}) collective-permute-start(bf16[1,1024,448]{1,2,0:T(8,128)(2,1)S(1)} %copy-done.13), channel_id=1, source_target_pairs={{32,0},{33,1},{34,2},{35,3},{36,4},{37,5},{38,6},{39,7},{40,8},{41... | collective-permute-start | bytes 2752520 | tf_op jit(solution)/shard_map/ppermute | solution.py:19
  80.7 62.7 %collective-permute-start = (bf16[1,448,1024]{2,1,0:T(8,128)(2,1)}, bf16[1,448,1024]{2,1,0:T(8,128)(2,1)}, u32[]{:S(2)}, u32[]{:S(2)}) collective-permute-start(bf16[1,448,1024]{2,1,0:T(8,128)(2,1)} %param.15), channel_id=1, source_target_pairs={{32,0},{33,1},{34,2},{35,3},{36,4},{37,5},{38,6},{39,7},{40,8},{41... | collective-permute-start | bytes 2752520 | tf_op jit(solution)/shard_map/ppermute | solution.py:19
  145.9 0.8 copy-start.2
  364.7 42.2 %all-to-all-start.3 = ((bf16[64,12,448]{2,1,0:T(8,128)(2,1)}), bf16[64,12,448]{2,1,0:T(8,128)(2,1)S(1)}, u32[]{:S(2)}, u32[]{:S(2)}) async-start(bf16[64,12,448]{2,1,0:T(8,128)(2,1)} %pad_maximum_fusion.1), calls=%async_computation.3 | async-start | bytes 2097152 | tf_op jit(solution)/shard_map/all_to_all | solution.py:141
  378.5 8.8 %copy-start.16 = (bf16[256,1024]{1,0:T(8,128)(2,1)S(1)}, bf16[256,1024]{1,0:T(8,128)(2,1)}, u32[]{:S(2)}) copy-start(bf16[256,1024]{1,0:T(8,128)(2,1)} %get-tuple-element.17) | copy-start | bytes 1572868
  382.1 9.7 %copy-start.10 = (bf16[512,1024]{1,0:T(8,128)(2,1)S(1)}, bf16[512,1024]{1,0:T(8,128)(2,1)}, u32[]{:S(2)}) copy-start(bf16[512,1024]{1,0:T(8,128)(2,1)} %get-tuple-element.19) | copy-start | bytes 3145732
  382.1 9.7 %copy-start.14 = (bf16[1,1024,448]{1,2,0:T(8,128)(2,1)S(1)}, bf16[1,1024,448]{1,2,0:T(8,128)(2,1)}, u32[]{:S(2)}) copy-start(bf16[1,1024,448]{1,2,0:T(8,128)(2,1)} %param.16) | copy-start | bytes 2752516
  382.1 124.8 %collective-permute-start.2 = (bf16[448,1024]{1,0:T(8,128)(2,1)}, bf16[448,1024]{1,0:T(8,128)(2,1)}, u32[]{:S(2)}, u32[]{:S(2)}) collective-permute-start(bf16[448,1024]{1,0:T(8,128)(2,1)} %get-tuple-element.24), channel_id=1, source_target_pairs={{0,32},{1,33},{2,34},{3,35},{4,36},{5,37},{6,38},{7,39},{8,40},{9,... | collective-permute-start | bytes 2752520 | tf_op jit(solution)/shard_map/ppermute | solution.py:19
  389.5 112.1 %collective-permute-start.3 = (bf16[1024,448]{0,1:T(8,128)(2,1)}, bf16[1024,448]{0,1:T(8,128)(2,1)}, u32[]{:S(2)}, u32[]{:S(2)}) collective-permute-start(bf16[1024,448]{0,1:T(8,128)(2,1)} %get-tuple-element.26), channel_id=1, source_target_pairs={{0,32},{1,33},{2,34},{3,35},{4,36},{5,37},{6,38},{7,39},{8,40},{9,... | collective-permute-start | bytes 2752520 | tf_op jit(solution)/shard_map/ppermute | solution.py:19
  406.9 108.8 %all-to-all-start.1 = ((bf16[64,12,448]{2,1,0:T(8,128)(2,1)}), bf16[64,12,448]{2,1,0:T(8,128)(2,1)S(1)}, u32[]{:S(2)}, u32[]{:S(2)}) async-start(bf16[64,12,448]{2,1,0:T(8,128)(2,1)} %pad_maximum_fusion), calls=%async_computation.1 | async-start | bytes 2097152 | tf_op jit(solution)/shard_map/all_to_all | solution.py:140
  501.6 5.3 copy-start.11
  501.6 5.3 copy-start.12
  501.6 5.3 copy-start.15
  501.6 5.3 copy-start.17
  516.1 4.0 copy-start.5
Sparse Core Ops, SparseCore 0:
  146.0 211.5 all-reduce.2
where the time goes:
time: 531 us; the launch traced here: 530 us
  waiting for transfers between devices  347 us (65%)
  starting transfers between devices  88.9 us (17%)
  matrix products  34.4 us (6%)
  other arithmetic  25.8 us (5%)
  local copies, waits for them, and re-layouts  19.4 us (4%)
  between operations  15.1 us (3%)
    psum x1, waiting for transfers between devices, dp_total(): lax.psum(tail_terms.astype(jnp.bfloat16), 'dp').astype(jnp.float32)  211 us
    ppermute x4, waiting for transfers between devices, shifted(): return lax.ppermute(block, axis, route)  77.6 us
    all_to_all x1, starting transfers between devices, shards(): lax.all_to_all(out_slots, 'expert', split_axis=0, concat_axis=0, tiled=True)  45.4 us
    all_to_all x1, waiting for transfers between devices, shards(): lax.all_to_all(send_feat, 'expert', split_axis=0, concat_axis=0, tiled=True)  26 us
    all_to_all x1, waiting for transfers between devices, shards(): lax.all_to_all(send_grad, 'expert', split_axis=0, concat_axis=0, tiled=True)  23.2 us
    another operation x3, other arithmetic  18.2 us
    dot_general x4, matrix products, outer_sum(): lax.dot_general(left_rows, right_rows, (((0,), (0,)), ((), ())), preferre...  15.3 us
    all_to_all x1, starting transfers between devices, shards(): lax.all_to_all(dx_slots, 'expert', split_axis=0, concat_axis=0, tiled=True)  13.8 us
  transfers between devices with their start and end apart: 9, of which 7 were waited for; matrix products, arithmetic and copies ran while one was open for 7% of the time, Pallas kernels for 0%

commit v1 on v0

v1 whole, which is shorter than its diff:
```python
import functools

import jax
import jax.numpy as jnp
from jax import lax
from jax.experimental import pallas as pl
from jax.experimental.pallas import tpu as pltpu
from jax.sharding import PartitionSpec as P

D = 3584
FFN = 1024
LOC = 448
WIDE = 2 * LOC
EXPERTS = 64
HALF = EXPERTS // 2
TOK = 128
COLD = 8
HOT = 16
COLD_ROWS = HALF * COLD
SLOTS = HALF * (COLD + HOT)
MAX_ROWS = EXPERTS * HOT
CR = 256
HR = CR // 2
NC = MAX_ROWS // CR
PLANE = 16
UP_SCALE = D ** -0.5
DOWN_SCALE = FFN ** -0.5
STEP = 4.0
NOISE = 0.25
F32 = jnp.float32
BF16 = jnp.bfloat16


def contract(a, b, da, db):
    return lax.dot_general(a, b, (((da,), (db,)), ((), ())), preferred_element_type=F32)


def stochastic(weights, grads, noise):
    target = weights.astype(F32) - STEP * grads
    return (target + (noise.astype(F32) - 0.5) * (NOISE * jnp.abs(target))).astype(BF16)


def kernel(
    both, ids_ref, probs_ref, cap_ref, up, down, noise,
    mixed, grad_tok, new_up, new_down,
    pick, phi, plo, packed, xg, ups, dnp, part, r1, r2, r3, ad, back, got, gup, gdn, noise_t,
    disp_send, disp_recv, step_send, step_recv, ret_send, ret_recv,
):
    dp = lax.axis_index("dp")
    me = lax.axis_index("expert")
    plane = me // PLANE
    inplane = lax.rem(me, PLANE)
    hot = me >= HALF
    x = lax.rem(dp, 4)
    z_hi = dp // 4
    bit_a = lax.rem((x + 1) // 2, 2)
    bit_b = x // 2
    peer_a = z_hi * 4 + (x + 1 - 2 * lax.rem(x, 2))
    peer_b = z_hi * 4 + (3 - x)
    peer_z = (1 - z_hi) * 4 + x

    barrier = pltpu.get_barrier_semaphore()

    @pl.loop(1, EXPERTS)
    def _(j):
        pl.semaphore_signal(barrier, inc=1, device_id=(dp, lax.rem(me + j, EXPERTS)),
                            device_id_type=pl.DeviceIdType.MESH)

    for peer in (peer_a, peer_b, peer_z):
        pl.semaphore_signal(barrier, inc=1, device_id=(peer, me),
                            device_id_type=pl.DeviceIdType.MESH)

    lanes_e = lax.broadcasted_iota(jnp.int32, (TOK, EXPERTS), 1)
    chosen = jnp.zeros((TOK, EXPERTS), F32)
    prob = jnp.zeros((TOK, EXPERTS), F32)
    for k in range(8):
        hit = ids_ref[:, k:k + 1] == lanes_e
        chosen = chosen + jnp.where(hit, 1.0, 0.0)
        prob = prob + jnp.where(hit, probs_ref[:, k:k + 1], 0.0)
    earlier = jnp.where(
        lax.broadcasted_iota(jnp.int32, (TOK, TOK), 0)
        > lax.broadcasted_iota(jnp.int32, (TOK, TOK), 1), 1.0, 0.0).astype(BF16)
    rank = jnp.dot(earlier, chosen.astype(BF16), preferred_element_type=F32)
    kept = jnp.where((chosen > 0.5) & (rank < cap_ref[...].astype(F32)), rank, -1.0).astype(BF16)
    prob_hi = prob.astype(BF16)
    prob_lo = (prob - prob_hi.astype(F32)).astype(BF16)
    for i in range(SLOTS // TOK):
        rows = pl.ds(i * TOK, TOK)
        r_e = lax.broadcasted_iota(jnp.int32, (TOK, EXPERTS), 0) + i * TOK
        r_t = lax.broadcasted_iota(jnp.int32, (TOK, TOK), 0) + i * TOK
        if i * TOK < COLD_ROWS:
            expert_of, slot_of = r_e // COLD, lax.rem(r_t, COLD)
        else:
            expert_of, slot_of = r_e // HOT + COLD_ROWS // HOT, lax.rem(r_t, HOT)
        spread = jnp.where(expert_of == lanes_e, 1.0, 0.0).astype(BF16)
        match = contract(spread, kept, 1, 1) == slot_of.astype(F32)
        sel = jnp.where(match, 1.0, 0.0).astype(BF16)
        w_hi = jnp.where(match, contract(spread, prob_hi, 1, 1), 0.0).astype(BF16)
        w_lo = jnp.where(match, contract(spread, prob_lo, 1, 1), 0.0).astype(BF16)
        pick[rows, :] = sel
        phi[rows, :] = w_hi
        plo[rows, :] = w_lo
        g = (jnp.dot(w_hi, both[:, 0:512], preferred_element_type=F32)
             + jnp.dot(w_lo, both[:, 0:512], preferred_element_type=F32))
        f = jnp.dot(sel, both[:, 384:WIDE], preferred_element_type=F32)
        lane = lax.broadcasted_iota(jnp.int32, (TOK, 128), 1)
        packed[rows, 0:384] = g[:, 0:384].astype(BF16)
        packed[rows, 384:512] = jnp.where(lane < 64, g[:, 384:512], f[:, 0:128]).astype(BF16)
        packed[rows, 512:WIDE] = f[:, 128:512].astype(BF16)

    pl.semaphore_wait(barrier, EXPERTS - 1 + 3)

    def send_plane(to_plane, count, first):
        @pl.loop(0, PLANE)
        def _(j):
            dest = to_plane * PLANE + lax.rem(inplane + j, PLANE)
            src = packed.at[pl.ds(pl.multiple_of(first + dest * count, 8), count)]
            dst = xg.at[pl.ds(pl.multiple_of(me * count, 8), count)]
            sem = disp_recv.at[(me * count) // CR]

            @pl.when(dest != me)
            def _():
                pltpu.make_async_remote_copy(
                    src_ref=src, dst_ref=dst, send_sem=disp_send, recv_sem=sem,
                    device_id=(dp, dest), device_id_type=pl.DeviceIdType.MESH).start()

            @pl.when(dest == me)
            def _():
                pltpu.make_async_copy(src, dst, sem).start()

    first_hot = jnp.where(hot, plane, 3 - plane)
    first_cold = jnp.where(hot, 3 - plane, plane)
    send_plane(first_hot, HOT, COLD_ROWS - HALF * HOT)
    send_plane(5 - first_hot, HOT, COLD_ROWS - HALF * HOT)
    send_plane(first_cold, COLD, 0)
    send_plane(1 - first_cold, COLD, 0)

    ups[0:64, :] = jnp.zeros((64, FFN), BF16)
    ups[64:512, :] = up[...]
    dnp[:, 384:512] = jnp.zeros((FFN, 128), BF16)
    dnp[:, 0:LOC] = down[...]

    def exchange(stage, q, h):
        first, second = (peer_a, peer_b) if h == 0 else (peer_b, peer_a)
        b1, b2 = (bit_a, bit_b) if h == 0 else (bit_b, bit_a)
        n1, n2, n3 = HR // 2, HR // 4, HR // 8
        if stage == 0:
            src, dst, peer = part.at[q, pl.ds(pl.multiple_of(n1 * (1 - b1), n1), n1)], r1.at[q], first
        elif stage == 1:
            src, dst, peer = r1.at[q, pl.ds(pl.multiple_of(n2 * (1 - b2), n2), n2)], r2.at[q], second
        elif stage == 2:
            src, dst, peer = r2.at[q, pl.ds(pl.multiple_of(n3 * (1 - z_hi), n3), n3)], r3.at[q], peer_z
        elif stage == 3:
            src = ad.at[q, pl.ds(pl.multiple_of(n1 * b1 + n2 * b2 + n3 * z_hi, n3), n3)]
            dst, peer = src, peer_z
        elif stage == 4:
            src = ad.at[q, pl.ds(pl.multiple_of(n1 * b1 + n2 * b2, n2), n2)]
            dst, peer = src, second
        else:
            src = ad.at[q, pl.ds(pl.multiple_of(n1 * b1, n1), n1)]
            dst, peer = src, first
        return pltpu.make_async_remote_copy(
            src_ref=src, dst_ref=dst, send_sem=step_send.at[stage, q],
            recv_sem=step_recv.at[stage, q], device_id=(peer, me),
            device_id_type=pl.DeviceIdType.MESH)

    chunks = jnp.where(hot, NC, NC // 2)

    def chunk_at(i):
        order = jnp.where(i == 0, plane, jnp.where(i == 1, 5 - plane, jnp.where(i == 2, 3 - plane, plane - 2)))
        return jnp.where(hot, order, i)

    def products_in(ci):
        whole = xg.at[pl.ds(pl.multiple_of(ci * CR, CR), CR)]
        pltpu.make_async_copy(whole, whole, disp_recv.at[ci]).wait()
        for h in range(2):
            q = ci * 2 + h
            rows = pl.ds(pl.multiple_of(ci * CR + h * HR, HR), HR)
            part[q, :, 0:FFN] = (contract(xg[rows, 384:WIDE], ups[...], 1, 0) * UP_SCALE).astype(BF16)
            part[q, :, FFN:2 * FFN] = (contract(xg[rows, 0:512], dnp[...], 1, 1) * DOWN_SCALE).astype(BF16)
            exchange(0, q, h).start()

    def add_first(ci):
        for h in range(2):
            q = ci * 2 + h
            n1 = HR // 2
            b1 = bit_a if h == 0 else bit_b
            exchange(0, q, h).wait_recv()
            keep = pl.ds(pl.multiple_of(n1 * b1, n1), n1)
            r1[q] = (r1[q].astype(F32) + part[q, keep, :].astype(F32)).astype(BF16)
            exchange(1, q, h).start()

    def add_second(ci):
        for h in range(2):
            q = ci * 2 + h
            n2 = HR // 4
            b2 = bit_b if h == 0 else bit_a
            exchange(1, q, h).wait_recv()
            keep = pl.ds(pl.multiple_of(n2 * b2, n2), n2)
            r2[q] = (r2[q].astype(F32) + r1[q, keep, :].astype(F32)).astype(BF16)
            exchange(2, q, h).start()

    def activate(ci):
        for h in range(2):
            q = ci * 2 + h
            n1, n2, n3 = HR // 2, HR // 4, HR // 8
            b1, b2 = (bit_a, bit_b) if h == 0 else (bit_b, bit_a)
            exchange(2, q, h).wait_recv()
            keep = pl.ds(pl.multiple_of(n3 * z_hi, n3), n3)
            total = r3[q].astype(F32) + r2[q, keep, :].astype(F32)
            pre, dact = total[:, 0:FFN], total[:, FFN:2 * FFN]
            s = 1.0 / (1.0 + jnp.exp(-pre))
            rows = pl.ds(pl.multiple_of(n1 * b1 + n2 * b2 + n3 * z_hi, n3), n3)
            ad[q, rows, 0:FFN] = (pre * s).astype(BF16)
            ad[q, rows, FFN:2 * FFN] = (dact * (s * (1.0 + pre * (1.0 - s)))).astype(BF16)
            exchange(3, q, h).start()

    def pass_on(stage, ci):
        for h in range(2):
            q = ci * 2 + h
            exchange(stage - 1, q, h).wait_recv()
            exchange(stage, q, h).start()

    def send_back(base, count, first):
        @pl.loop(0, HR // count)
        def _(j):
            dest = base // count + j
            src = back.at[pl.ds(pl.multiple_of(base + j * count, 8), count)]
            dst = got.at[pl.ds(pl.multiple_of(first + me * count, 8), count)]

            @pl.when(dest != me)
            def _():
                pltpu.make_async_remote_copy(
                    src_ref=src, dst_ref=dst, send_sem=ret_send, recv_sem=ret_recv,
                    device_id=(dp, dest), device_id_type=pl.DeviceIdType.MESH).start()

            @pl.when(dest == me)
            def _():
                pltpu.make_async_copy(src, dst, ret_recv).start()

    def products_out(ci):
        for h in range(2):
            q = ci * 2 + h
            base = ci * CR + h * HR
            rows = pl.ds(pl.multiple_of(base, HR), HR)
            exchange(5, q, h).wait_recv()
            y = contract(ad[q, :, 0:FFN], dnp[...], 1, 0) * DOWN_SCALE
            d = contract(ad[q, :, FFN:2 * FFN], ups[...], 1, 1) * UP_SCALE
            back[rows, 0:384] = y[:, 0:384].astype(BF16)
            back[rows, 384:512] = (y[:, 384:512] + d[:, 0:128]).astype(BF16)
            back[rows, 512:WIDE] = d[:, 128:512].astype(BF16)

            @pl.when(hot)
            def _():
                send_back(base, HOT, COLD_ROWS - HALF * HOT)

            @pl.when(jnp.logical_not(hot))
            def _():
                send_back(base, COLD, 0)

        for h in range(2):
            q = ci * 2 + h
            rows = pl.ds(pl.multiple_of(ci * CR + h * HR, HR), HR)

            @pl.loop(0, FFN // 256)
            def _(t):
                cols = pl.ds(pl.multiple_of(t * 256, 256), 256)
                cols_d = pl.ds(pl.multiple_of(FFN + t * 256, 256), 256)
                gup[:, cols] += contract(xg[rows, 384:WIDE], ad[q, :, cols_d], 0, 0)
                gdn[cols, :] += contract(ad[q, :, cols], xg[rows, 0:512], 0, 0)

    gup[...] = jnp.zeros_like(gup)
    gdn[...] = jnp.zeros_like(gdn)
    eye = jnp.where(
        lax.broadcasted_iota(jnp.int32, (128, 128), 0)
        == lax.broadcasted_iota(jnp.int32, (128, 128), 1), 1.0, 0.0).astype(BF16)

    @pl.loop(0, FFN // 128)
    def _(t):
        cols = pl.ds(pl.multiple_of(t * 128, 128), 128)
        noise_t[cols, :] = contract(eye, noise[:, cols], 1, 1).astype(BF16)

    stages = [
        products_in, add_first, add_second, activate,
        functools.partial(pass_on, 4), functools.partial(pass_on, 5), products_out,
    ]

    @pl.loop(0, chunks + len(stages) - 1)
    def _(t):
        for s in reversed(range(len(stages))):
            i = t - s

            @pl.when((i >= 0) & (i < chunks))
            def _(s=s, i=i):
                stages[s](chunk_at(i))

    @pl.loop(0, 7)
    def _(t):
        rows = pl.ds(pl.multiple_of(t * 64, 64), 64)
        rows_g = pl.ds(pl.multiple_of(t * 64 + 64, 64), 64)
        new_up[rows, :] = stochastic(up[rows, :], UP_SCALE * gup[rows_g, :], noise[rows, :])

    @pl.loop(0, 8)
    def _(t):
        rows = pl.ds(pl.multiple_of(t * 128, 128), 128)
        new_down[rows, :] = stochastic(down[rows, :], DOWN_SCALE * gdn[rows, 0:LOC], noise_t[rows, :])

    pltpu.make_async_copy(got, got, ret_recv).wait()
    m = contract(phi[...], got[:, 0:512], 0, 0) + contract(plo[...], got[:, 0:512], 0, 0)
    mixed[...] = m[:, 0:LOC].astype(BF16)
    grad_tok[...] = contract(pick[...], got[:, 384:WIDE], 0, 0).astype(BF16)

    @pl.loop(0, chunks)
    def _(c):
        for h in range(2):
            for stage in range(6):
                exchange(stage, c * 2 + h, h).wait_send()

    def drain(sent, returned):
        a = packed.at[pl.ds(0, sent)]
        pltpu.make_async_copy(a, a, disp_send).wait()
        b = back.at[pl.ds(0, returned)]
        pltpu.make_async_copy(b, b, ret_send).wait()

    @pl.when(hot)
    def _():
        drain(SLOTS - HOT, EXPERTS * HOT - HOT)

    @pl.when(jnp.logical_not(hot))
    def _():
        drain(SLOTS - COLD, EXPERTS * COLD - COLD)


def shards(
    features, upstream, expert_ids, gate_probs, capacity, up_weight, down_weight, round_noise
):
    both = jnp.concatenate([upstream, features], axis=1)
    vmem = pl.BlockSpec(memory_space=pltpu.VMEM)
    shape = jax.ShapeDtypeStruct
    mixed, grad_tok, new_up, new_down = pl.pallas_call(
        kernel,
        out_shape=(
            shape((TOK, LOC), BF16), shape((TOK, 512), BF16),
            shape((LOC, FFN), BF16), shape((FFN, LOC), BF16),
        ),
        in_specs=[vmem] * 7,
        out_specs=(vmem,) * 4,
        scratch_shapes=[
            pltpu.VMEM((SLOTS, TOK), BF16),
            pltpu.VMEM((SLOTS, TOK), BF16),
            pltpu.VMEM((SLOTS, TOK), BF16),
            pltpu.VMEM((SLOTS, WIDE), BF16),
            pltpu.VMEM((MAX_ROWS, WIDE), BF16),
            pltpu.VMEM((512, FFN), BF16),
            pltpu.VMEM((FFN, 512), BF16),
            pltpu.VMEM((2 * NC, HR, 2 * FFN), BF16),
            pltpu.VMEM((2 * NC, HR // 2, 2 * FFN), BF16),
            pltpu.VMEM((2 * NC, HR // 4, 2 * FFN), BF16),
            pltpu.VMEM((2 * NC, HR // 8, 2 * FFN), BF16),
            pltpu.VMEM((2 * NC, HR, 2 * FFN), BF16),
            pltpu.VMEM((MAX_ROWS, WIDE), BF16),
            pltpu.VMEM((SLOTS, WIDE), BF16),
            pltpu.VMEM((512, FFN), F32),
            pltpu.VMEM((FFN, 512), F32),
            pltpu.VMEM((FFN, LOC), BF16),
            pltpu.SemaphoreType.DMA,
            pltpu.SemaphoreType.DMA((NC,)),
            pltpu.SemaphoreType.DMA((6, 2 * NC)),
            pltpu.SemaphoreType.DMA((6, 2 * NC)),
            pltpu.SemaphoreType.DMA,
            pltpu.SemaphoreType.DMA,
        ],
        compiler_params=pltpu.CompilerParams(
            collective_id=0, has_side_effects=True, vmem_limit_bytes=56 * 1024 * 1024),
    )(both, expert_ids, gate_probs, capacity.reshape(1, EXPERTS),
      up_weight[0], down_weight[0], round_noise[0])
    return mixed, grad_tok[:, 64:], new_up[None], new_down[None]


def solution(mesh):
    in_specs = (
        P("expert", "dp"),
        P("expert", "dp"),
        P("expert", None),
        P("expert", None),
        P(),
        P("expert", "dp", None),
        P("expert", None, "dp"),
        P("expert", "dp", None),
    )
    out_specs = (
        P("expert", "dp"),
        P("expert", "dp"),
        P("expert", "dp", None),
        P("expert", None, "dp"),
    )
    return jax.shard_map(shards, mesh=mesh, in_specs=in_specs, out_specs=out_specs, check_vma=False)
```

time: 531 us -> 179 us (0.34)
  the two profiles are of different devices: /device:TPU:65 before, /device:TPU:369 now
where the time goes in v1:
time: 179 us
  Pallas kernels  166 us (93%)
  local copies, waits for them, and re-layouts  12 us (7%)
    pallas_call x1, Pallas kernels, shards(): pl.pallas_call(kernel, out_shape=(shape((TOK, LOC), BF16), shape((TOK, 51...  166 us
    unnamed x15, local copies, waits for them, and re-layouts  11.9 us

profile of v1, /device:TPU:369, one launch (start us, length us, event | category | flops | bytes accessed | tf_op | source)
XLA Modules:
  0.0 179.1 jit_solution(3238677166700896272)
XLA Ops:
  0.6 0.0 copy-start.1
  0.6 1.5 copy.15.ids_ref
  2.1 1.4 copy.16.probs_ref
  3.6 1.0 copy.13
  4.6 1.0 copy.12
  5.6 0.8 pad_maximum_fusion.both
  6.4 0.0 copy-done.1
  6.4 1.3 copy.14
  7.7 165.6 %shard_map.111 = (bf16[128,448]{1,0:T(8,128)(2,1)}, bf16[128,512]{1,0:T(8,128)(2,1)}, bf16[448,1024]{1,0:T(8,128)(2,1)}, bf16[1024,448]{1,0:T(8,128)(2,1)}) custom-call(bf16[128,896]{1,0:T(8,128)(2,1)} %pad_maximum_fusion.both, s32[128,8]{1,0:T(8,128)} %copy.15.ids_ref, f32[128,8]{1,0:T(8,128)} %copy.16.probs_ref, s32[1,64]{1,0:T(1,128)} %bitcast.11, ...), custom_call_target="tpu_custom_call" | custom-call | tf_op jit(solution)/shard_map/pallas_call | solution.py:340
  173.3 0.0 copy-start.2
  173.3 1.7 copy.17
  175.0 0.0 copy-done.2
  175.0 0.1 slice.3
  175.1 0.8 copy.18
  175.9 0.0 copy-start
  175.9 2.3 %copy.19 = bf16[1,1024,448]{1,2,0:T(8,128)(2,1)} copy(bf16[1,1024,448]{2,1,0:T(8,128)(2,1)} %bitcast.7) | data formatting | bytes 1835008
  178.2 0.0 copy-done
  178.2 0.9 copy.21
Async XLA Ops:
  0.6 5.7 %copy-start.1 = (bf16[1,1024,448]{1,2,0:T(8,128)(2,1)S(1)}, bf16[1,1024,448]{1,2,0:T(8,128)(2,1)}, u32[]{:S(2)}) copy-start(bf16[1,1024,448]{1,2,0:T(8,128)(2,1)} %param.14) | copy-start | bytes 2752516
  173.3 1.7 copy-start.2
  175.9 2.3 %copy-start = (bf16[448,1024]{1,0:T(8,128)(2,1)S(1)}, bf16[448,1024]{1,0:T(8,128)(2,1)}, u32[]{:S(2)}) copy-start(bf16[448,1024]{1,0:T(8,128)(2,1)} %get-tuple-element.10) | copy-start | bytes 2752516

commit v2 on v0

v2 whole, which is shorter than its diff:
```python
import jax
import jax.numpy as jnp
from jax import lax
from jax.experimental import pallas as pl
from jax.experimental.pallas import tpu as pltpu
from jax.sharding import PartitionSpec as P

D = 3584
FFN = 1024
LOC = 448
WIDE = 2 * LOC
EXPERTS = 64
HALF = EXPERTS // 2
TOK = 128
COLD = 8
HOT = 16
MAX_ROWS = EXPERTS * HOT
CR = 128
QR = CR // 4
NC = MAX_ROWS // CR
PAD = 512
PLANE = 16
PLANES = EXPERTS // PLANE
UP_SCALE = D ** -0.5
DOWN_SCALE = FFN ** -0.5
STEP = 4.0
NOISE = 0.25
F32 = jnp.float32
BF16 = jnp.bfloat16


def contract(a, b, da, db):
    return lax.dot_general(a, b, (((da,), (db,)), ((), ())), preferred_element_type=F32)


def stochastic(weights, grads, noise):
    target = weights.astype(F32) - STEP * grads
    return (target + (noise.astype(F32) - 0.5) * (NOISE * jnp.abs(target))).astype(BF16)


def kernel(
    feat, cot, ids_ref, probs_ref, cap_ref, up_hbm, down_hbm, noise_hbm,
    mixed, grad_tok, new_up, new_down,
    fpad, cpad, ids_all, probs_all, pick, phi, plo, packed, xg, ups, dnp, noise, part, r1, r2, r3,
    ad, back, got, half_out, sums,
    load_sem, share_send, share_recv, disp_send, disp_recv, step_send, step_recv, ret_send, ret_recv,
    sum_send, sum_recv,
):
    dp = lax.axis_index("dp")
    me = lax.axis_index("expert")
    plane = me // PLANE
    inplane = lax.rem(me, PLANE)
    hot = me >= HALF
    x = lax.rem(dp, 4)
    z_hi = dp // 4
    bit_a = lax.rem((x + 1) // 2, 2)
    bit_b = x // 2
    peer_a = z_hi * 4 + (x + 1 - 2 * lax.rem(x, 2))
    peer_b = z_hi * 4 + (3 - x)
    peer_z = (1 - z_hi) * 4 + x

    barrier = pltpu.get_barrier_semaphore()

    def other_plane(d):
        return lax.rem(plane + d, PLANES)

    @pl.loop(1, PLANE)
    def _(j):
        pl.semaphore_signal(barrier, inc=1,
                            device_id=(dp, plane * PLANE + lax.rem(inplane + j, PLANE)),
                            device_id_type=pl.DeviceIdType.MESH)

    @pl.loop(1, PLANES)
    def _(d):
        pl.semaphore_signal(barrier, inc=1, device_id=(dp, other_plane(d) * PLANE + inplane),
                            device_id_type=pl.DeviceIdType.MESH)

    for peer in (peer_a, peer_b, peer_z):
        pl.semaphore_signal(barrier, inc=1, device_id=(peer, me),
                            device_id_type=pl.DeviceIdType.MESH)

    loads = [
        pltpu.make_async_copy(up_hbm, ups.at[pl.ds(64, LOC)], load_sem.at[0]),
        pltpu.make_async_copy(down_hbm, dnp.at[pl.ds(0, LOC)], load_sem.at[1]),
        pltpu.make_async_copy(noise_hbm, noise, load_sem.at[2]),
    ]
    for load in loads:
        load.start()

    for p in range(PLANES):
        fpad[p, 0:64, :] = jnp.zeros((64, TOK), BF16)
        cpad[p, LOC:PAD, :] = jnp.zeros((64, TOK), BF16)
    fpad[plane, 64:PAD, :] = feat[...]
    cpad[plane, 0:LOC, :] = cot[...]
    ids_all[plane] = ids_ref[...]
    probs_all[plane] = probs_ref[...]

    def share(d):
        to = other_plane(d)
        pairs = ((ids_ref, ids_all.at[plane]), (probs_ref, probs_all.at[plane]),
                 (cot, cpad.at[plane, pl.ds(0, LOC)]), (feat, fpad.at[plane, pl.ds(64, LOC)]))
        return [pltpu.make_async_remote_copy(
            src_ref=src, dst_ref=dst, send_sem=share_send.at[n, d], recv_sem=share_recv.at[n, d],
            device_id=(dp, to * PLANE + inplane), device_id_type=pl.DeviceIdType.MESH)
            for n, (src, dst) in enumerate(pairs)]

    def source(k):
        return jnp.where(k == 0, plane, jnp.where(
            k == 1, plane + 1 - 2 * lax.rem(plane, 2),
            jnp.where(k == 2, lax.rem(plane + 2, PLANES), 3 - plane)))

    pl.semaphore_wait(barrier, PLANE - 1 + PLANES - 1 + 3)
    for k in range(1, PLANES):
        for copy in share(lax.rem(source(k) - plane + PLANES, PLANES)):
            copy.start()

    row_e = lax.broadcasted_iota(jnp.int32, (EXPERTS, TOK), 0)
    earlier = jnp.where(
        lax.broadcasted_iota(jnp.int32, (TOK, TOK), 0)
        < lax.broadcasted_iota(jnp.int32, (TOK, TOK), 1), 1.0, 0.0).astype(BF16)
    diagonal = (lax.broadcasted_iota(jnp.int32, (EXPERTS, EXPERTS), 0)
                == lax.broadcasted_iota(jnp.int32, (EXPERTS, EXPERTS), 1))
    limit = jnp.sum(jnp.where(diagonal, cap_ref[...].astype(F32), 0.0), axis=1, keepdims=True)

    def pack(p, count):
        chosen = jnp.zeros((EXPERTS, TOK), F32)
        prob = jnp.zeros((EXPERTS, TOK), F32)
        for k in range(8):
            hit = ids_all[p, k:k + 1, :] == row_e
            chosen = chosen + jnp.where(hit, 1.0, 0.0)
            prob = prob + jnp.where(hit, probs_all[p, k:k + 1, :], 0.0)
        rank = jnp.dot(chosen.astype(BF16), earlier, preferred_element_type=F32)
        kept = jnp.where((chosen > 0.5) & (rank < limit), rank, -1.0).astype(BF16)
        prob_hi = prob.astype(BF16)
        prob_lo = (prob - prob_hi.astype(F32)).astype(BF16)
        for i in range(PLANE * count // TOK):
            rows = pl.ds(i * TOK, TOK)
            r_e = lax.broadcasted_iota(jnp.int32, (TOK, EXPERTS), 0) + i * TOK
            lane_e = lax.broadcasted_iota(jnp.int32, (TOK, EXPERTS), 1)
            slot_of = lax.rem(lax.broadcasted_iota(jnp.int32, (TOK, TOK), 0), count)
            spread = jnp.where(r_e // count + plane * PLANE == lane_e, 1.0, 0.0).astype(BF16)
            match = contract(spread, kept, 1, 0) == slot_of.astype(F32)
            sel = jnp.where(match, 1.0, 0.0).astype(BF16)
            w_hi = jnp.where(match, contract(spread, prob_hi, 1, 0), 0.0).astype(BF16)
            w_lo = jnp.where(match, contract(spread, prob_lo, 1, 0), 0.0).astype(BF16)
            pick[p, rows, :] = sel
            phi[p, rows, :] = w_hi
            plo[p, rows, :] = w_lo
            g = contract(w_hi, cpad[p], 1, 1) + contract(w_lo, cpad[p], 1, 1)
            f = contract(sel, fpad[p], 1, 1)
            packed[p, rows, 0:384] = g[:, 0:384].astype(BF16)
            packed[p, rows, 384:512] = (g[:, 384:512] + f[:, 0:128]).astype(BF16)
            packed[p, rows, 512:WIDE] = f[:, 128:512].astype(BF16)

        block = p * PLANE + inplane

        @pl.loop(0, PLANE)
        def _(j):
            place = lax.rem(inplane + j, PLANE)
            src = packed.at[p, pl.ds(pl.multiple_of(place * count, 8), count)]
            dst = xg.at[pl.ds(pl.multiple_of(block * count, 8), count)]
            sem = disp_recv.at[(block * count) // CR]

            @pl.when(place != inplane)
            def _():
                pltpu.make_async_remote_copy(
                    src_ref=src, dst_ref=dst, send_sem=disp_send, recv_sem=sem,
                    device_id=(dp, plane * PLANE + place),
                    device_id_type=pl.DeviceIdType.MESH).start()

            @pl.when(place == inplane)
            def _():
                pltpu.make_async_copy(src, dst, sem).start()

    def pack_any(p):
        @pl.when(hot)
        def _():
            pack(p, HOT)

        @pl.when(jnp.logical_not(hot))
        def _():
            pack(p, COLD)

    pack_any(plane)

    def pack_next(i):
        @pl.when(i < PLANES - 1)
        def _():
            p = source(i + 1)
            d = lax.rem(plane - p + PLANES, PLANES)
            for copy in share(d):
                copy.wait_recv()
            pack_any(p)

    ups[0:64, :] = jnp.zeros((64, FFN), BF16)
    dnp[LOC:PAD, :] = jnp.zeros((64, FFN), BF16)
    for load in loads:
        load.wait()

    def remote(src, dst, stage, c, w, peer):
        return pltpu.make_async_remote_copy(
            src_ref=src, dst_ref=dst, send_sem=step_send.at[stage, c, w],
            recv_sem=step_recv.at[stage, c, w], device_id=(peer, me),
            device_id_type=pl.DeviceIdType.MESH)

    def copies(stage, c):
        if stage == 0:
            return [remote(part.at[c, 0, 1 - bit_a], r1.at[c, 0], 0, c, 0, peer_a),
                    remote(part.at[c, 1, :, 1 - bit_b], r1.at[c, 1], 0, c, 1, peer_b)]
        if stage == 1:
            return [remote(r1.at[c, 0, 1 - bit_b], r2.at[c, 0], 1, c, 0, peer_b),
                    remote(r1.at[c, 1, 1 - bit_a], r2.at[c, 1], 1, c, 1, peer_a)]
        if stage == 2:
            return [remote(r2.at[c], r3.at[c], 2, c, 0, peer_z)]
        if stage == 3:
            q0, q1 = ad.at[0, c, bit_a, bit_b], ad.at[1, c, bit_a, bit_b]
            return [remote(q0, q0, 3, c, 0, peer_b), remote(q1, q1, 3, c, 1, peer_a)]
        h0, h1 = ad.at[0, c, bit_a], ad.at[1, c, :, bit_b]
        return [remote(h0, h0, 4, c, 0, peer_a), remote(h1, h1, 4, c, 1, peer_b)]

    def start(stage, c):
        for copy in copies(stage, c):
            copy.start()

    def arrived(stage, c):
        for copy in copies(stage, c):
            copy.wait_recv()

    def add(u, v):
        return (u.astype(F32) + v.astype(F32)).astype(BF16)

    chunks = jnp.where(hot, NC, NC // 2)

    def chunk_at(i):
        return jnp.where(hot, source(i // 2) * 2 + lax.rem(i, 2), source(i))

    def products_in(i):
        c = chunk_at(i)
        rows = pl.ds(pl.multiple_of(c * CR, CR), CR)
        pltpu.make_async_copy(xg.at[rows], xg.at[rows], disp_recv.at[c]).wait()
        shape = (2, 2, QR, FFN)
        pre = contract(xg[rows, 384:WIDE], ups[...], 1, 0) * UP_SCALE
        part[c, 0] = pre.astype(BF16).reshape(shape)
        dact = contract(xg[rows, 0:PAD], dnp[...], 1, 0) * DOWN_SCALE
        part[c, 1] = dact.astype(BF16).reshape(shape)
        start(0, c)

    def add_first(i):
        c = chunk_at(i)
        arrived(0, c)
        r1[c, 0] = add(r1[c, 0], part[c, 0, bit_a])
        for a in range(2):
            r1[c, 1, a] = add(r1[c, 1, a], part[c, 1, a, bit_b])
        start(1, c)

    def add_second(i):
        c = chunk_at(i)
        arrived(1, c)
        r2[c, 0] = add(r2[c, 0], r1[c, 0, bit_b])
        r2[c, 1] = add(r2[c, 1], r1[c, 1, bit_a])
        start(2, c)

    def activate(i):
        c = chunk_at(i)
        arrived(2, c)
        pre = r3[c, 0].astype(F32) + r2[c, 0].astype(F32)
        dact = r3[c, 1].astype(F32) + r2[c, 1].astype(F32)
        s = 1.0 / (1.0 + jnp.exp(-pre))
        ad[0, c, bit_a, bit_b] = (pre * s).astype(BF16)
        ad[1, c, bit_a, bit_b] = (dact * (s * (1.0 + pre * (1.0 - s)))).astype(BF16)
        start(3, c)

    def pass_half(i):
        c = chunk_at(i)
        arrived(3, c)
        start(4, c)

    def send_back(c, count):
        per = CR // count

        @pl.loop(0, per)
        def _(j):
            block = c * per + j
            p, place = block // PLANE, lax.rem(block, PLANE)
            src = back.at[pl.ds(pl.multiple_of(block * count, 8), count)]
            dst = got.at[p, pl.ds(pl.multiple_of(inplane * count, 8), count)]

            @pl.when(place != inplane)
            def _():
                pltpu.make_async_remote_copy(
                    src_ref=src, dst_ref=dst, send_sem=ret_send, recv_sem=ret_recv.at[p],
                    device_id=(dp, plane * PLANE + place),
                    device_id_type=pl.DeviceIdType.MESH).start()

            @pl.when(place == inplane)
            def _():
                pltpu.make_async_copy(src, dst, ret_recv.at[p]).start()

    def products_out(i):
        c = chunk_at(i)
        arrived(4, c)
        base = c * CR
        rows = pl.ds(pl.multiple_of(base, CR), CR)
        y = contract(ad[0, c].reshape(CR, FFN), dnp[...], 1, 1) * DOWN_SCALE
        d = contract(ad[1, c].reshape(CR, FFN), ups[...], 1, 1) * UP_SCALE
        back[rows, 0:384] = y[:, 0:384].astype(BF16)
        back[rows, 384:512] = (y[:, 384:512] + d[:, 0:128]).astype(BF16)
        back[rows, 512:WIDE] = d[:, 128:512].astype(BF16)

        @pl.when(hot)
        def _():
            send_back(c, HOT)

        @pl.when(jnp.logical_not(hot))
        def _():
            send_back(c, COLD)

    def total_copy(d):
        to = other_plane(d)
        return pltpu.make_async_remote_copy(
            src_ref=half_out.at[to], dst_ref=sums.at[plane], send_sem=sum_send.at[d],
            recv_sem=sum_recv.at[d], device_id=(dp, to * PLANE + inplane),
            device_id_type=pl.DeviceIdType.MESH)

    def combine(p, count):
        n = PLANE * count
        rows = got.at[p, pl.ds(0, n)]
        pltpu.make_async_copy(rows, rows, ret_recv.at[p]).wait()
        out = got[p, 0:n, 0:PAD]
        m = contract(out, phi[p, 0:n, :], 0, 0) + contract(out, plo[p, 0:n, :], 0, 0)
        half_out[p, 0] = m[0:LOC, :].astype(BF16)
        g = contract(got[p, 0:n, 384:WIDE], pick[p, 0:n, :], 0, 0)
        half_out[p, 1] = g[64:PAD, :].astype(BF16)

        @pl.when(p != plane)
        def _():
            total_copy(lax.rem(p - plane + PLANES, PLANES)).start()

    def combine_next(i):
        @pl.when(hot & (lax.rem(i, 2) == 1))
        def _():
            combine(source(i // 2), HOT)

        @pl.when(jnp.logical_not(hot))
        def _():
            combine(source(i), COLD)

    schedule = [
        (add_first, 1), (activate, 2), (products_in, 0), (add_second, 1), (products_out, 3),
        (pass_half, 2), (pack_next, 0), (combine_next, 5),
    ]
    lag_max = max(lag for _, lag in schedule)

    @pl.loop(0, chunks + lag_max)
    def _(t):
        for stage, lag in schedule:
            i = t - lag

            @pl.when((i >= 0) & (i < chunks))
            def _(stage=stage, i=i):
                stage(i)

    def update(count):
        n = count // CR
        act = ad[0, 0:n].reshape(count, FFN)
        dpre = ad[1, 0:n].reshape(count, FFN)
        for i in range(4):
            lo, hi = i * 128, i * 128 + 128
            grad = contract(xg[0:count, 384 + lo:384 + hi], dpre, 0, 0)
            skip = 64 if i == 0 else 0
            new_up[lo + skip - 64:hi - 64, :] = stochastic(
                ups[lo + skip:hi, :], UP_SCALE * grad[skip:, :], noise[lo + skip - 64:hi - 64, :])
            grad = contract(xg[0:count, lo:hi], act, 0, 0)
            hi = min(hi, LOC)
            new_down[lo:hi, :] = stochastic(
                dnp[lo:hi, :], DOWN_SCALE * grad[0:hi - lo, :], noise[lo:hi, :])

    @pl.when(hot)
    def _():
        update(MAX_ROWS)

    @pl.when(jnp.logical_not(hot))
    def _():
        update(EXPERTS * COLD)

    m = half_out[plane, 0].astype(F32)
    g = half_out[plane, 1].astype(F32)
    for d in range(1, PLANES):
        total_copy(d).wait_recv()
        p = lax.rem(plane - d + PLANES, PLANES)
        m = m + sums[p, 0].astype(F32)
        g = g + sums[p, 1].astype(F32)
    mixed[...] = m.astype(BF16)
    grad_tok[...] = g.astype(BF16)

    @pl.loop(0, chunks)
    def _(c):
        for stage in range(5):
            for copy in copies(stage, c):
                copy.wait_send()

    for d in range(1, PLANES):
        total_copy(d).wait_send()
        for copy in share(d):
            copy.wait_send()

    def drain(count):
        sent = back.at[pl.ds(0, PLANES * (PLANE - 1) * count)]
        pltpu.make_async_copy(sent, sent, disp_send).wait()
        pltpu.make_async_copy(sent, sent, ret_send).wait()

    @pl.when(hot)
    def _():
        drain(HOT)

    @pl.when(jnp.logical_not(hot))
    def _():
        drain(COLD)


def shards(
    features, upstream, expert_ids, gate_probs, capacity, up_weight, down_weight, round_noise
):
    vmem = pl.BlockSpec(memory_space=pltpu.VMEM)
    hbm = pl.BlockSpec(memory_space=pl.ANY)
    shape = jax.ShapeDtypeStruct
    mixed, grad_tok, new_up, new_down = pl.pallas_call(
        kernel,
        out_shape=(
            shape((LOC, TOK), BF16), shape((LOC, TOK), BF16),
            shape((LOC, FFN), BF16), shape((LOC, FFN), BF16),
        ),
        in_specs=[vmem] * 5 + [hbm] * 3,
        out_specs=(vmem,) * 4,
        scratch_shapes=[
            pltpu.VMEM((PLANES, PAD, TOK), BF16),
            pltpu.VMEM((PLANES, PAD, TOK), BF16),
            pltpu.VMEM((PLANES, 8, TOK), jnp.int32),
            pltpu.VMEM((PLANES, 8, TOK), F32),
            pltpu.VMEM((PLANES, PLANE * HOT, TOK), BF16),
            pltpu.VMEM((PLANES, PLANE * HOT, TOK), BF16),
            pltpu.VMEM((PLANES, PLANE * HOT, TOK), BF16),
            pltpu.VMEM((PLANES, PLANE * HOT, WIDE), BF16),
            pltpu.VMEM((MAX_ROWS, WIDE), BF16),
            pltpu.VMEM((PAD, FFN), BF16),
            pltpu.VMEM((PAD, FFN), BF16),
            pltpu.VMEM((LOC, FFN), BF16),
            pltpu.VMEM((NC, 2, 2, 2, QR, FFN), BF16),
            pltpu.VMEM((NC, 2, 2, QR, FFN), BF16),
            pltpu.VMEM((NC, 2, QR, FFN), BF16),
            pltpu.VMEM((NC, 2, QR, FFN), BF16),
            pltpu.VMEM((2, NC, 2, 2, QR, FFN), BF16),
            pltpu.VMEM((MAX_ROWS, WIDE), BF16),
            pltpu.VMEM((PLANES, PLANE * HOT, WIDE), BF16),
            pltpu.VMEM((PLANES, 2, LOC, TOK), BF16),
            pltpu.VMEM((PLANES, 2, LOC, TOK), BF16),
            pltpu.SemaphoreType.DMA((3,)),
            pltpu.SemaphoreType.DMA((4, PLANES)),
            pltpu.SemaphoreType.DMA((4, PLANES)),
            pltpu.SemaphoreType.DMA,
            pltpu.SemaphoreType.DMA((NC,)),
            pltpu.SemaphoreType.DMA((5, NC, 2)),
            pltpu.SemaphoreType.DMA((5, NC, 2)),
            pltpu.SemaphoreType.DMA,
            pltpu.SemaphoreType.DMA((PLANES,)),
            pltpu.SemaphoreType.DMA((PLANES,)),
            pltpu.SemaphoreType.DMA((PLANES,)),
        ],
        compiler_params=pltpu.CompilerParams(
            collective_id=0, has_side_effects=True, vmem_limit_bytes=56 * 1024 * 1024),
    )(features.T, upstream.T, expert_ids.T, gate_probs.T, capacity.reshape(1, EXPERTS),
      up_weight[0], down_weight[0].T, round_noise[0])
    return mixed.T, grad_tok.T, new_up[None], new_down.T[None]


def solution(mesh):
    in_specs = (
        P("expert", "dp"),
        P("expert", "dp"),
        P("expert", None),
        P("expert", None),
        P(),
        P("expert", "dp", None),
        P("expert", None, "dp"),
        P("expert", "dp", None),
    )
    out_specs = (
        P("expert", "dp"),
        P("expert", "dp"),
        P("expert", "dp", None),
        P("expert", None, "dp"),
    )
    return jax.shard_map(shards, mesh=mesh, in_specs=in_specs, out_specs=out_specs, check_vma=False)
```

time: 531 us -> 146 us (0.27)
  the two profiles are of different devices: /device:TPU:65 before, /device:TPU:120 now
where the time goes in v2:
time: 146 us
  Pallas kernels  140 us (96%)
  local copies, waits for them, and re-layouts  5.4 us (4%)
    pallas_call x1, Pallas kernels, shards(): pl.pallas_call(kernel, out_shape=(shape((LOC, TOK), BF16), shape((LOC, TO...  140 us
    unnamed x8, local copies, waits for them, and re-layouts  5.4 us

profile of v2, /device:TPU:120, one launch (start us, length us, event | category | flops | bytes accessed | tf_op | source)
XLA Modules:
  0.0 145.6 jit_solution(1146721295026262585)
XLA Ops:
  0.6 139.6 %shard_map.111 = (bf16[448,128]{1,0:T(8,128)(2,1)}, bf16[448,128]{1,0:T(8,128)(2,1)}, bf16[448,1024]{1,0:T(8,128)(2,1)}, bf16[448,1024]{1,0:T(8,128)(2,1)}) custom-call(bf16[448,128]{1,0:T(8,128)(2,1)} %bitcast.23, bf16[448,128]{1,0:T(8,128)(2,1)} %bitcast.24, s32[8,128]{1,0:T(8,128)} %bitcast.25, f32[8,128]{1,0:T(8,128)} %bitcast.26, s32[1,64]{1,0:T(1,128)} %bitcast.27, ...), custom_call_target="tpu_custom_call" | custom-call | tf_op jit(solution)/shard_map/pallas_call | solution.py:427
  140.2 0.0 copy-start.1
  140.2 1.6 %copy.16 = bf16[128,448]{0,1:T(8,128)(2,1)} copy(bf16[128,448]{0,1:T(8,128)(2,1)} %bitcast.22) | data formatting | bytes 229376
  141.8 0.0 copy-done.1
  141.8 0.6 copy.17
  142.5 0.0 copy-start
  142.5 2.2 %copy.18 = bf16[1,448,1024]{2,1,0:T(8,128)(2,1)} copy(bf16[1,448,1024]{2,1,0:T(8,128)(2,1)} %bitcast.17) | data formatting | bytes 1835008
  144.7 0.0 copy-done
  144.7 0.9 copy.19
Async XLA Ops:
  140.2 1.6 %copy-start.1 = (bf16[448,128]{1,0:T(8,128)(2,1)S(1)}, bf16[448,128]{1,0:T(8,128)(2,1)}, u32[]{:S(2)}) copy-start(bf16[448,128]{1,0:T(8,128)(2,1)} %get-tuple-element.9) | copy-start | bytes 344068
  142.5 2.2 %copy-start = (bf16[448,1024]{1,0:T(8,128)(2,1)S(1)}, bf16[448,1024]{1,0:T(8,128)(2,1)}, u32[]{:S(2)}) copy-start(bf16[448,1024]{1,0:T(8,128)(2,1)} %get-tuple-element.11) | copy-start | bytes 2752516

commit v3 on v2

--- a/solution.py
+++ b/solution.py
@@ -108,11 +108,6 @@
         return jnp.where(k == 0, plane, jnp.where(
             k == 1, plane + 1 - 2 * lax.rem(plane, 2),
             jnp.where(k == 2, lax.rem(plane + 2, PLANES), 3 - plane)))
-
-    pl.semaphore_wait(barrier, PLANE - 1 + PLANES - 1 + 3)
-    for k in range(1, PLANES):
-        for copy in share(lax.rem(source(k) - plane + PLANES, PLANES)):
-            copy.start()
 
     row_e = lax.broadcasted_iota(jnp.int32, (EXPERTS, TOK), 0)
     earlier = jnp.where(
@@ -152,6 +147,7 @@
             packed[p, rows, 384:512] = (g[:, 384:512] + f[:, 0:128]).astype(BF16)
             packed[p, rows, 512:WIDE] = f[:, 128:512].astype(BF16)
 
+    def send_block(p, count):
         block = p * PLANE + inplane
 
         @pl.loop(0, PLANE)
@@ -172,16 +168,21 @@
             def _():
                 pltpu.make_async_copy(src, dst, sem).start()
 
-    def pack_any(p):
+    def by_kind(work, *operands):
         @pl.when(hot)
         def _():
-            pack(p, HOT)
+            work(*operands, HOT)
 
         @pl.when(jnp.logical_not(hot))
         def _():
-            pack(p, COLD)
-
-    pack_any(plane)
+            work(*operands, COLD)
+
+    by_kind(pack, plane)
+    pl.semaphore_wait(barrier, PLANE - 1 + PLANES - 1 + 3)
+    by_kind(send_block, plane)
+    for k in range(1, PLANES):
+        for copy in share(lax.rem(source(k) - plane + PLANES, PLANES)):
+            copy.start()
 
     def pack_next(i):
         @pl.when(i < PLANES - 1)
@@ -190,7 +191,8 @@
             d = lax.rem(plane - p + PLANES, PLANES)
             for copy in share(d):
                 copy.wait_recv()
-            pack_any(p)
+            by_kind(pack, p)
+            by_kind(send_block, p)
 
     ups[0:64, :] = jnp.zeros((64, FFN), BF16)
     dnp[LOC:PAD, :] = jnp.zeros((64, FFN), BF16)
@@ -198,7 +200,7 @@
         load.wait()
 
     def remote(src, dst, stage, c, w, peer):
-        return pltpu.make_async_remote_copy(
+        return lambda: pltpu.make_async_remote_copy(
             src_ref=src, dst_ref=dst, send_sem=step_send.at[stage, c, w],
             recv_sem=step_recv.at[stage, c, w], device_id=(peer, me),
             device_id_type=pl.DeviceIdType.MESH)
@@ -220,11 +222,17 @@
 
     def start(stage, c):
         for copy in copies(stage, c):
-            copy.start()
+            copy().start()
+
+    def start_one(stage, c, w):
+        copies(stage, c)[w]().start()
 
     def arrived(stage, c):
         for copy in copies(stage, c):
-            copy.wait_recv()
+            copy().wait_recv()
+
+    def arrived_one(stage, c, w):
+        copies(stage, c)[w]().wait_recv()
 
     def add(u, v):
         return (u.astype(F32) + v.astype(F32)).astype(BF16)
@@ -241,17 +249,20 @@
         shape = (2, 2, QR, FFN)
         pre = contract(xg[rows, 384:WIDE], ups[...], 1, 0) * UP_SCALE
         part[c, 0] = pre.astype(BF16).reshape(shape)
+        start_one(0, c, 0)
         dact = contract(xg[rows, 0:PAD], dnp[...], 1, 0) * DOWN_SCALE
         part[c, 1] = dact.astype(BF16).reshape(shape)
-        start(0, c)
+        start_one(0, c, 1)
 
     def add_first(i):
         c = chunk_at(i)
-        arrived(0, c)
+        arrived_one(0, c, 0)
         r1[c, 0] = add(r1[c, 0], part[c, 0, bit_a])
+        start_one(1, c, 0)
+        arrived_one(0, c, 1)
         for a in range(2):
             r1[c, 1, a] = add(r1[c, 1, a], part[c, 1, a, bit_b])
-        start(1, c)
+        start_one(1, c, 1)
 
     def add_second(i):
         c = chunk_at(i)
@@ -272,8 +283,9 @@
 
     def pass_half(i):
         c = chunk_at(i)
-        arrived(3, c)
-        start(4, c)
+        for w in range(2):
+            arrived_one(3, c, w)
+            start_one(4, c, w)
 
     def send_back(c, count):
         per = CR // count
@@ -347,9 +359,9 @@
 
     schedule = [
         (add_first, 1), (activate, 2), (products_in, 0), (add_second, 1), (products_out, 3),
-        (pass_half, 2), (pack_next, 0), (combine_next, 5),
+        (pass_half, 2), (pack_next, 0), (combine_next, 4),
     ]
-    lag_max = max(lag for _, lag in schedule)
+    lag_max = 3
 
     @pl.loop(0, chunks + lag_max)
     def _(t):
@@ -360,28 +372,28 @@
             def _(stage=stage, i=i):
                 stage(i)
 
-    def update(count):
-        n = count // CR
-        act = ad[0, 0:n].reshape(count, FFN)
-        dpre = ad[1, 0:n].reshape(count, FFN)
-        for i in range(4):
-            lo, hi = i * 128, i * 128 + 128
+    def update_up(slots):
+        count = EXPERTS * slots
+        dpre = ad[1, 0:count // CR].reshape(count, FFN)
+        for lo in range(0, PAD, 128):
+            hi = lo + 128
             grad = contract(xg[0:count, 384 + lo:384 + hi], dpre, 0, 0)
-            skip = 64 if i == 0 else 0
+            skip = 64 if lo == 0 else 0
             new_up[lo + skip - 64:hi - 64, :] = stochastic(
                 ups[lo + skip:hi, :], UP_SCALE * grad[skip:, :], noise[lo + skip - 64:hi - 64, :])
-            grad = contract(xg[0:count, lo:hi], act, 0, 0)
-            hi = min(hi, LOC)
+
+    def update_down(slots):
+        count = EXPERTS * slots
+        act = ad[0, 0:count // CR].reshape(count, FFN)
+        for lo in range(0, PAD, 128):
+            grad = contract(xg[0:count, lo:lo + 128], act, 0, 0)
+            hi = min(lo + 128, LOC)
             new_down[lo:hi, :] = stochastic(
                 dnp[lo:hi, :], DOWN_SCALE * grad[0:hi - lo, :], noise[lo:hi, :])
 
-    @pl.when(hot)
-    def _():
-        update(MAX_ROWS)
-
-    @pl.when(jnp.logical_not(hot))
-    def _():
-        update(EXPERTS * COLD)
+    by_kind(update_up)
+    combine_next(chunks - 1)
+    by_kind(update_down)
 
     m = half_out[plane, 0].astype(F32)
     g = half_out[plane, 1].astype(F32)
@@ -397,7 +409,7 @@
     def _(c):
         for stage in range(5):
             for copy in copies(stage, c):
-                copy.wait_send()
+                copy().wait_send()
 
     for d in range(1, PLANES):
         total_copy(d).wait_send()

time: 146 us -> 144 us (0.986)
  Pallas kernels: 140 us -> 138 us
    pallas_call x1, Pallas kernels: 140 us -> 138 us  [shards(): pl.pallas_call(kernel, out_shape=(shape((LOC, TOK), BF16), shape((LOC, TO...]
where the time goes in v3:
time: 144 us
  Pallas kernels  138 us (96%)
  local copies, waits for them, and re-layouts  5.4 us (4%)
    pallas_call x1, Pallas kernels, shards(): pl.pallas_call(kernel, out_shape=(shape((LOC, TOK), BF16), shape((LOC, TO...  138 us
    unnamed x8, local copies, waits for them, and re-layouts  5.4 us

profile of v3, /device:TPU:120, one launch (start us, length us, event | category | flops | bytes accessed | tf_op | source)
XLA Modules:
  0.0 143.7 jit_solution(16284179825553228955)
XLA Ops:
  0.6 137.6 %shard_map.111 = (bf16[448,128]{1,0:T(8,128)(2,1)}, bf16[448,128]{1,0:T(8,128)(2,1)}, bf16[448,1024]{1,0:T(8,128)(2,1)}, bf16[448,1024]{1,0:T(8,128)(2,1)}) custom-call(bf16[448,128]{1,0:T(8,128)(2,1)} %bitcast.23, bf16[448,128]{1,0:T(8,128)(2,1)} %bitcast.24, s32[8,128]{1,0:T(8,128)} %bitcast.25, f32[8,128]{1,0:T(8,128)} %bitcast.26, s32[1,64]{1,0:T(1,128)} %bitcast.27, ...), custom_call_target="tpu_custom_call" | custom-call | tf_op jit(solution)/shard_map/pallas_call | solution.py:439
  138.2 0.0 copy-start.1
  138.3 1.6 %copy.16 = bf16[128,448]{0,1:T(8,128)(2,1)} copy(bf16[128,448]{0,1:T(8,128)(2,1)} %bitcast.22) | data formatting | bytes 229376
  139.8 0.0 copy-done.1
  139.8 0.6 copy.17
  140.5 0.0 copy-start
  140.5 2.2 %copy.18 = bf16[1,448,1024]{2,1,0:T(8,128)(2,1)} copy(bf16[1,448,1024]{2,1,0:T(8,128)(2,1)} %bitcast.17) | data formatting | bytes 1835008
  142.7 0.0 copy-done
  142.7 0.9 copy.19
Async XLA Ops:
  138.2 1.6 %copy-start.1 = (bf16[448,128]{1,0:T(8,128)(2,1)S(1)}, bf16[448,128]{1,0:T(8,128)(2,1)}, u32[]{:S(2)}) copy-start(bf16[448,128]{1,0:T(8,128)(2,1)} %get-tuple-element.9) | copy-start | bytes 344068
  140.5 2.2 %copy-start = (bf16[448,1024]{1,0:T(8,128)(2,1)S(1)}, bf16[448,1024]{1,0:T(8,128)(2,1)}, u32[]{:S(2)}) copy-start(bf16[448,1024]{1,0:T(8,128)(2,1)} %get-tuple-element.11) | copy-start | bytes 2752516

commit v4 on v3

--- a/solution.py
+++ b/solution.py
@@ -278,8 +278,9 @@
         dact = r3[c, 1].astype(F32) + r2[c, 1].astype(F32)
         s = 1.0 / (1.0 + jnp.exp(-pre))
         ad[0, c, bit_a, bit_b] = (pre * s).astype(BF16)
+        start_one(3, c, 0)
         ad[1, c, bit_a, bit_b] = (dact * (s * (1.0 + pre * (1.0 - s)))).astype(BF16)
-        start(3, c)
+        start_one(3, c, 1)
 
     def pass_half(i):
         c = chunk_at(i)

time: 144 us -> 144 us (level)
  no operation moved by 1% of the time
where the time goes in v4:
time: 144 us
  Pallas kernels  137 us (95%)
  local copies, waits for them, and re-layouts  5.4 us (4%)
    pallas_call x1, Pallas kernels, shards(): pl.pallas_call(kernel, out_shape=(shape((LOC, TOK), BF16), shape((LOC, TO...  137 us
    unnamed x8, local copies, waits for them, and re-layouts  5.4 us

profile of v4, /device:TPU:120, one launch (start us, length us, event | category | flops | bytes accessed | tf_op | source)
XLA Modules:
  0.0 143.5 jit_solution(13158285009621370074)
XLA Ops:
  0.6 137.5 %shard_map.111 = (bf16[448,128]{1,0:T(8,128)(2,1)}, bf16[448,128]{1,0:T(8,128)(2,1)}, bf16[448,1024]{1,0:T(8,128)(2,1)}, bf16[448,1024]{1,0:T(8,128)(2,1)}) custom-call(bf16[448,128]{1,0:T(8,128)(2,1)} %bitcast.23, bf16[448,128]{1,0:T(8,128)(2,1)} %bitcast.24, s32[8,128]{1,0:T(8,128)} %bitcast.25, f32[8,128]{1,0:T(8,128)} %bitcast.26, s32[1,64]{1,0:T(1,128)} %bitcast.27, ...), custom_call_target="tpu_custom_call" | custom-call | tf_op jit(solution)/shard_map/pallas_call | solution.py:440
  138.1 0.0 copy-start.1
  138.1 1.6 %copy.16 = bf16[128,448]{0,1:T(8,128)(2,1)} copy(bf16[128,448]{0,1:T(8,128)(2,1)} %bitcast.22) | data formatting | bytes 229376
  139.7 0.0 copy-done.1
  139.7 0.6 copy.17
  140.4 0.0 copy-start
  140.4 2.2 %copy.18 = bf16[1,448,1024]{2,1,0:T(8,128)(2,1)} copy(bf16[1,448,1024]{2,1,0:T(8,128)(2,1)} %bitcast.17) | data formatting | bytes 1835008
  142.6 0.0 copy-done
  142.6 0.9 copy.19
Async XLA Ops:
  138.1 1.6 %copy-start.1 = (bf16[448,128]{1,0:T(8,128)(2,1)S(1)}, bf16[448,128]{1,0:T(8,128)(2,1)}, u32[]{:S(2)}) copy-start(bf16[448,128]{1,0:T(8,128)(2,1)} %get-tuple-element.9) | copy-start | bytes 344068
  140.4 2.2 %copy-start = (bf16[448,1024]{1,0:T(8,128)(2,1)S(1)}, bf16[448,1024]{1,0:T(8,128)(2,1)}, u32[]{:S(2)}) copy-start(bf16[448,1024]{1,0:T(8,128)(2,1)} %get-tuple-element.11) | copy-start | bytes 2752516
